TPU v7x, 32 devices: a whole 2x2x4 slice. The times are simulated.
32 devices in a mesh: ctx: 8 (over z, x), ch: 4 (over y, core).
Axes of the slice: x: 2, y: 2, z: 4, core: 2. Of those that a mesh axis runs over, the one named last changes fastest.
Arguments:
- query_input: bfloat16 [4096, 4096], P('ch', 'ctx'), may hold values from -6 to 6
- key_input: bfloat16 [4096, 4096], P('ch', 'ctx'), may hold values from -6 to 6
- value_input: bfloat16 [4096, 4096], P('ch', 'ctx'), may hold values from -6 to 6
- decay_rate: float32 [8, 16], P('ch'), may hold values from 0 to 1, as said below
- residue: float32 [8, 16], P('ch'), may hold values from -1 to 1
- doc_ends: int32 [4], replicated, may hold values from 1 to 4096, as said below
- out_weight: bfloat16 [4096, 4096], P(None, 'ch'), may hold values from -0.09375 to 0.09375
- out_cotangent: bfloat16 [4096, 4096], P('ctx', 'ch'), may hold values from -6 to 6
Outputs:
- query_grad: bfloat16 [4096, 4096], P('ch', 'ctx')
- key_grad: bfloat16 [4096, 4096], P('ch', 'ctx')
- value_grad: bfloat16 [4096, 4096], P('ch', 'ctx')
- weight_grad: float32 [4096, 4096], P('ctx', 'ch')
Inputs may be any that keep to these rules, and one draw needn't show every extreme that they name: `doc_ends`: strictly increasing; the last entry equals 4096. `decay_rate`: positive.
All inputs are finite; a program needn't handle non-finite values.
Results may differ from a plain program's by a relative error of at most 0.0029.
Values may be sent and summed in bfloat16 or wider, within the bound.
A program may use at most 128 MiB of HBM per device.

v0:
```python
import math
import jax
import jax.numpy as jnp
from jax import lax
from jax.sharding import PartitionSpec as P


def passed_along(block, axis, distance):
    devices = range(lax.axis_size(axis))
    route = [(i - distance, i) for i in devices if i - distance in devices]
    return lax.ppermute(block, axis, route)


def local(
    query_input, key_input, value_input, decay_rate, residue, doc_ends, out_weight, out_cotangent
):
    rows_here, length = query_input.shape
    groups = decay_rate.shape[0]
    group_rows = rows_here // groups
    shard_index = lax.axis_index("ctx")
    anchor = shard_index * length
    offsets = jnp.arange(length, dtype=jnp.int32)
    positions = anchor + offsets
    doc_ids = jnp.sum((doc_ends[None, :] <= positions[:, None]).astype(jnp.int32), axis=1)
    previous = jnp.where(shard_index > 0, jnp.sum((doc_ends <= anchor - 1).astype(jnp.int32)), -1)
    row_block = out_weight
    output_grad = lax.psum_scatter(
        lax.dot_general(
            row_block, out_cotangent, (((1,), (1,)), ((), ())), preferred_element_type=jnp.float32
        ),
        "ch",
        scatter_dimension=0,
        tiled=True,
    )
    highest = lax.Precision.HIGHEST
    place = offsets.astype(jnp.float32)
    centre = place - 0.5 * length
    rising = jnp.exp(-centre[None, :, None] * decay_rate[:, None, :]) * residue[:, None, :]
    falling = jnp.exp(centre[None, :, None] * decay_rate[:, None, :])
    kernel = jnp.einsum("gtn,gsn->gts", rising, falling, precision=highest)
    causal = (offsets[:, None] >= offsets[None, :]) & (doc_ids[:, None] == doc_ids[None, :])
    kernel = jnp.where(causal[None, :, :], kernel, 0.0)
    alive_mask = (doc_ids == previous).astype(jnp.float32)
    tail_mask = (doc_ids == doc_ids[-1]).astype(jnp.float32)
    carry_in_map = (
        residue[:, :, None]
        * jnp.exp(-decay_rate[:, :, None] * (place + 1.0)[None, None, :])
        * alive_mask[None, None, :]
    )
    carry_out_map = (
        jnp.exp(-decay_rate[:, :, None] * (length - 1.0 - place)[None, None, :])
        * tail_mask[None, None, :]
    )
    back_out_map = (
        jnp.exp(-decay_rate[:, :, None] * place[None, None, :]) * alive_mask[None, None, :]
    )
    back_in_map = (
        residue[:, :, None]
        * jnp.exp(-decay_rate[:, :, None] * (length - place)[None, None, :])
        * tail_mask[None, None, :]
    )
    transit = jnp.exp(-decay_rate * length) * (doc_ids[-1] == previous).astype(jnp.float32)
    query_f = query_input.astype(jnp.float32)
    key_f = key_input.astype(jnp.float32)
    value_f = value_input.astype(jnp.float32)
    mixed = (key_f * value_f).reshape(groups, group_rows, length)
    signal = (output_grad * query_f).reshape(groups, group_rows, length)
    forward_part = jnp.einsum("gnl,gcl->gnc", carry_out_map, mixed, precision=highest)
    backward_part = jnp.einsum("gnl,gcl->gnc", back_out_map, signal, precision=highest)

    def chain_turn(turn_index, carried):
        ahead, behind = carried
        ahead = passed_along(transit[:, :, None] * ahead + forward_part, "ctx", 1)
        behind = passed_along(transit[:, :, None] * behind + backward_part, "ctx", -1)
        return (ahead, behind)

    start_pair = (jnp.zeros_like(forward_part), jnp.zeros_like(backward_part))
    entering, returning = lax.fori_loop(0, lax.axis_size("ctx") - 1, chain_turn, start_pair)
    filtered = jnp.einsum("gcs,gts->gct", mixed, kernel, precision=highest)
    filtered = filtered + jnp.einsum("gnc,gnt->gct", entering, carry_in_map, precision=highest)
    spread = jnp.einsum("gct,gts->gcs", signal, kernel, precision=highest)
    spread = spread + jnp.einsum("gnc,gns->gcs", returning, back_in_map, precision=highest)
    filtered = filtered.reshape(rows_here, length)
    spread = spread.reshape(rows_here, length)
    gated = (query_f * filtered).astype(jnp.bfloat16)
    query_grad = (output_grad * filtered).astype(jnp.bfloat16)
    key_grad = (spread * value_f).astype(jnp.bfloat16)
    value_grad = (spread * key_f).astype(jnp.bfloat16)
    gathered = lax.all_gather(gated, "ch", axis=0, tiled=True)
    norm_factor = 1.0 / math.sqrt(length * lax.axis_size("ctx"))
    row_block = gathered
    weight_grad = lax.psum_scatter(
        jnp.dot(row_block, out_cotangent, preferred_element_type=jnp.float32) * norm_factor,
        "ctx",
        scatter_dimension=0,
        tiled=True,
    )
    return (query_grad, key_grad, value_grad, weight_grad)


def solution(mesh):
    return jax.shard_map(
        local,
        mesh=mesh,
        in_specs=(
            P("ch", "ctx"),
            P("ch", "ctx"),
            P("ch", "ctx"),
            P("ch", None),
            P("ch", None),
            P(),
            P(None, "ch"),
            P("ctx", "ch"),
        ),
        out_specs=(P("ch", "ctx"), P("ch", "ctx"), P("ch", "ctx"), P("ctx", "ch")),
        check_vma=False,
    )
```

profile of v0, /device:TPU:0, one launch (start us, length us, event | category | flops | bytes accessed | tf_op | source)
XLA Modules:
  0.0 521.5 jit_solution(614125705850805751)
XLA Ops:
  7.2 1.2 copy-done
  8.4 10.2 %fusion.70 = f32[4096,512]{1,0:T(8,128)} fusion(bf16[4096,1024]{1,0:T(8,128)(2,1)} %param.16, bf16[512,1024]{1,0:T(8,128)(2,1)S(1)} %copy-done), kind=kOutput, calls=%fused_computation.83 | convolution fusion | flops 4294967296 | bytes 17825792 | tf_op jit(solution)/shard_map/dot_general | solution.py:28
  23.4 3.3 fusion.37
  27.0 1.3 copy-done.1
  28.3 2.5 fusion.33
  30.8 62.4 %reduce-scatter.3.cloned.1.call-done = f32[1024,512]{1,0:T(8,128)} async-done(((f32[4096,512]{1,0:T(8,128)}), f32[1024,512]{1,0:T(8,128)}) %reduce-scatter.3.cloned.1.call-update) | async-done | bytes 2097168 | tf_op jit(solution)/shard_map/reduce_scatter | solution.py:27
  93.3 2.2 convert_multiply_fusion.1
  95.4 2.5 fusion.29
  97.9 82.0 %while.12 = (s32[]{:T(128)}, f32[2,16,512]{2,1,0:T(8,128)S(1)}, f32[2,16,512]{2,1,0:T(8,128)S(1)}, f32[2,16]{1,0:T(2,128)S(1)}, f32[2,16,512]{2,1,0:T(8,128)}, /*index=5*/f32[2,16,512]{2,1,0:T(8,128)}, s32[]{:T(128)}) while((s32[]{:T(128)}, f32[2,16,512]{2,1,0:T(8,128)S(1)}, f32[2,16,512]{2,1,0:T(8,128)S(1)}, f32[2,16]{1,0:T(2,128)S(1)}, ...), condition=%wide.region_4.5_spmd, body=%wide.region_3.4_spmd.sunk | while | flops 65538 | bytes 917789 | solution.py:78
  98.0 1.6 multiply_add_fusion.3
  99.5 3.3 collective-permute-start
  102.9 1.3 collective-permute-start.1
  105.1 4.2 collective-permute-done.1
  109.3 1.6 multiply_add_fusion.3
  110.9 4.3 collective-permute-start
  115.2 1.3 collective-permute-start.1
  116.5 0.9 collective-permute-done
  117.4 4.2 collective-permute-done.1
  121.5 1.6 multiply_add_fusion.3
  123.1 3.4 collective-permute-start
  126.5 1.3 collective-permute-start.1
  127.8 1.5 collective-permute-done
  129.3 3.6 collective-permute-done.1
  132.8 1.6 multiply_add_fusion.3
  134.4 4.3 collective-permute-start
  138.7 1.3 collective-permute-start.1
  140.9 4.2 collective-permute-done.1
  145.1 1.6 multiply_add_fusion.3
  146.7 3.4 collective-permute-start
  150.0 1.3 collective-permute-start.1
  152.2 4.2 collective-permute-done.1
  156.4 1.6 multiply_add_fusion.3
  158.0 4.4 collective-permute-start
  162.4 1.3 collective-permute-start.1
  164.6 4.2 collective-permute-done.1
  168.7 1.6 multiply_add_fusion.3
  170.3 3.3 collective-permute-start
  173.6 1.3 collective-permute-start.1
  175.8 4.2 collective-permute-done.1
  180.0 2.7 fusion.24
  182.7 5.4 %fusion.8 = f32[2,512,512]{2,1,0:T(8,128)S(1)} fusion(f32[2,512,512]{2,1,0:T(8,128)S(1)} %fusion.24, f32[2,512,512]{2,1,0:T(8,128)S(1)} %bitcast.24, f32[2,512,512]{2,1,0:T(8,128)} %fusion.37, pred[512,512]{1,0:T(8,128)(4,1)S(1)} %fusion.16), kind=kOutput, calls=%fused_computation.17 | convolution fusion | flops 3222274048 | bytes 8650752 | tf_op jit(solution)/shard_map/gcs,gts->gct/dot_general | solution.py:79
  188.1 2.0 fusion.2
  190.4 31.3 %all-gather.2.cloned.1.call-done = bf16[4096,512]{1,0:T(8,128)(2,1)} async-done(((bf16[1024,512]{1,0:T(8,128)(2,1)}), bf16[4096,512]{1,0:T(8,128)(2,1)}) %all-gather.2.cloned.1.call-update) | async-done | bytes 4194320 | tf_op jit(solution)/shard_map/all_gather | solution.py:89
  221.7 10.3 %broadcast_multiply_fusion = f32[4096,1024]{1,0:T(8,128)} fusion(bf16[4096,512]{1,0:T(8,128)(2,1)} %all-gather.2.cloned.1.call-done, bf16[512,1024]{1,0:T(8,128)(2,1)S(1)} %copy-done), kind=kOutput, calls=%fused_computation.2 | convolution fusion | flops 4299161600 | bytes 22020096 | tf_op jit(solution)/shard_map/dot_general | solution.py:93
  232.7 1.9 fusion.19
  234.6 3.7 fusion.11
  238.3 1.8 fusion
  240.1 274.8 %reduce-scatter.5.cloned.1.call-done = f32[512,1024]{1,0:T(8,128)} async-done(((f32[4096,1024]{1,0:T(8,128)}), f32[512,1024]{1,0:T(8,128)}) %reduce-scatter.5.cloned.1.call-update) | async-done | bytes 2097168 | tf_op jit(solution)/shard_map/reduce_scatter | solution.py:92
  (52 shorter events, 9.2 us)
Async XLA Ops:
  7.2 1.2 copy-start
  7.2 86.1 %reduce-scatter.3.cloned.1.call-start = ((), (), s32[]{:S(2)}) async-start(), calls=%async_computation.2 | async-start | bytes 10485760 | tf_op jit(solution)/shard_map/reduce_scatter | solution.py:27
  18.6 0.7 copy-start.13
  18.6 3.8 copy-start.12
  18.6 4.7 copy-start.10
  18.7 8.0 %copy-start.6 = (bf16[1024,512]{1,0:T(8,128)(2,1)S(1)}, bf16[1024,512]{1,0:T(8,128)(2,1)}, u32[]{:S(2)}) copy-start(bf16[1024,512]{1,0:T(8,128)(2,1)} %param.12) | copy-start | bytes 3145732
  18.7 8.0 %copy-start.8 = (bf16[1024,512]{1,0:T(8,128)(2,1)S(1)}, bf16[1024,512]{1,0:T(8,128)(2,1)}, u32[]{:S(2)}) copy-start(bf16[1024,512]{1,0:T(8,128)(2,1)} %param.11) | copy-start | bytes 3145732
  18.7 203.0 %all-gather.2.cloned.1.call-start = ((), (), s32[]{:S(2)}) async-start(), calls=%async_computation.3 | async-start | bytes 5242880 | tf_op jit(solution)/shard_map/all_gather | solution.py:89
  27.0 1.3 copy-start.1
  99.5 5.6 %collective-permute-start = (f32[2,16,512]{2,1,0:T(8,128)}, f32[2,16,512]{2,1,0:T(8,128)S(1)}, u32[]{:S(2)}, u32[]{:S(2)}) collective-permute-start(f32[2,16,512]{2,1,0:T(8,128)} %get-tuple-element.102), channel_id=1, source_target_pairs={{0,4},{4,8},{8,12},{12,16},{16,20},{20,24},{24,28},{1,5},{5,9},{9,... | collective-permute-start | bytes 196616 | tf_op jit(solution)/shard_map/while/body/eval_jaxpr/ppermute | solution.py:11
  102.9 6.4 %collective-permute-start.1 = (f32[2,16,512]{2,1,0:T(8,128)}, f32[2,16,512]{2,1,0:T(8,128)S(1)}, u32[]{:S(2)}, u32[]{:S(2)}) collective-permute-start(f32[2,16,512]{2,1,0:T(8,128)} %get-tuple-element.103), channel_id=1, source_target_pairs={{4,0},{8,4},{12,8},{16,12},{20,16},{24,20},{28,24},{5,1},{9,5},{13... | collective-permute-start | bytes 196616 | tf_op jit(solution)/shard_map/while/body/eval_jaxpr/ppermute | solution.py:11
  110.9 6.5 %collective-permute-start = (f32[2,16,512]{2,1,0:T(8,128)}, f32[2,16,512]{2,1,0:T(8,128)S(1)}, u32[]{:S(2)}, u32[]{:S(2)}) collective-permute-start(f32[2,16,512]{2,1,0:T(8,128)} %get-tuple-element.102), channel_id=1, source_target_pairs={{0,4},{4,8},{8,12},{12,16},{16,20},{20,24},{24,28},{1,5},{5,9},{9,... | collective-permute-start | bytes 196616 | tf_op jit(solution)/shard_map/while/body/eval_jaxpr/ppermute | solution.py:11
  115.2 6.4 %collective-permute-start.1 = (f32[2,16,512]{2,1,0:T(8,128)}, f32[2,16,512]{2,1,0:T(8,128)S(1)}, u32[]{:S(2)}, u32[]{:S(2)}) collective-permute-start(f32[2,16,512]{2,1,0:T(8,128)} %get-tuple-element.103), channel_id=1, source_target_pairs={{4,0},{8,4},{12,8},{16,12},{20,16},{24,20},{28,24},{5,1},{9,5},{13... | collective-permute-start | bytes 196616 | tf_op jit(solution)/shard_map/while/body/eval_jaxpr/ppermute | solution.py:11
  123.1 6.2 %collective-permute-start = (f32[2,16,512]{2,1,0:T(8,128)}, f32[2,16,512]{2,1,0:T(8,128)S(1)}, u32[]{:S(2)}, u32[]{:S(2)}) collective-permute-start(f32[2,16,512]{2,1,0:T(8,128)} %get-tuple-element.102), channel_id=1, source_target_pairs={{0,4},{4,8},{8,12},{12,16},{16,20},{20,24},{24,28},{1,5},{5,9},{9,... | collective-permute-start | bytes 196616 | tf_op jit(solution)/shard_map/while/body/eval_jaxpr/ppermute | solution.py:11
  126.5 6.4 %collective-permute-start.1 = (f32[2,16,512]{2,1,0:T(8,128)}, f32[2,16,512]{2,1,0:T(8,128)S(1)}, u32[]{:S(2)}, u32[]{:S(2)}) collective-permute-start(f32[2,16,512]{2,1,0:T(8,128)} %get-tuple-element.103), channel_id=1, source_target_pairs={{4,0},{8,4},{12,8},{16,12},{20,16},{24,20},{28,24},{5,1},{9,5},{13... | collective-permute-start | bytes 196616 | tf_op jit(solution)/shard_map/while/body/eval_jaxpr/ppermute | solution.py:11
  134.4 6.5 %collective-permute-start = (f32[2,16,512]{2,1,0:T(8,128)}, f32[2,16,512]{2,1,0:T(8,128)S(1)}, u32[]{:S(2)}, u32[]{:S(2)}) collective-permute-start(f32[2,16,512]{2,1,0:T(8,128)} %get-tuple-element.102), channel_id=1, source_target_pairs={{0,4},{4,8},{8,12},{12,16},{16,20},{20,24},{24,28},{1,5},{5,9},{9,... | collective-permute-start | bytes 196616 | tf_op jit(solution)/shard_map/while/body/eval_jaxpr/ppermute | solution.py:11
  138.7 6.4 %collective-permute-start.1 = (f32[2,16,512]{2,1,0:T(8,128)}, f32[2,16,512]{2,1,0:T(8,128)S(1)}, u32[]{:S(2)}, u32[]{:S(2)}) collective-permute-start(f32[2,16,512]{2,1,0:T(8,128)} %get-tuple-element.103), channel_id=1, source_target_pairs={{4,0},{8,4},{12,8},{16,12},{20,16},{24,20},{28,24},{5,1},{9,5},{13... | collective-permute-start | bytes 196616 | tf_op jit(solution)/shard_map/while/body/eval_jaxpr/ppermute | solution.py:11
  146.7 5.6 %collective-permute-start = (f32[2,16,512]{2,1,0:T(8,128)}, f32[2,16,512]{2,1,0:T(8,128)S(1)}, u32[]{:S(2)}, u32[]{:S(2)}) collective-permute-start(f32[2,16,512]{2,1,0:T(8,128)} %get-tuple-element.102), channel_id=1, source_target_pairs={{0,4},{4,8},{8,12},{12,16},{16,20},{20,24},{24,28},{1,5},{5,9},{9,... | collective-permute-start | bytes 196616 | tf_op jit(solution)/shard_map/while/body/eval_jaxpr/ppermute | solution.py:11
  150.0 6.4 %collective-permute-start.1 = (f32[2,16,512]{2,1,0:T(8,128)}, f32[2,16,512]{2,1,0:T(8,128)S(1)}, u32[]{:S(2)}, u32[]{:S(2)}) collective-permute-start(f32[2,16,512]{2,1,0:T(8,128)} %get-tuple-element.103), channel_id=1, source_target_pairs={{4,0},{8,4},{12,8},{16,12},{20,16},{24,20},{28,24},{5,1},{9,5},{13... | collective-permute-start | bytes 196616 | tf_op jit(solution)/shard_map/while/body/eval_jaxpr/ppermute | solution.py:11
  158.0 6.6 %collective-permute-start = (f32[2,16,512]{2,1,0:T(8,128)}, f32[2,16,512]{2,1,0:T(8,128)S(1)}, u32[]{:S(2)}, u32[]{:S(2)}) collective-permute-start(f32[2,16,512]{2,1,0:T(8,128)} %get-tuple-element.102), channel_id=1, source_target_pairs={{0,4},{4,8},{8,12},{12,16},{16,20},{20,24},{24,28},{1,5},{5,9},{9,... | collective-permute-start | bytes 196616 | tf_op jit(solution)/shard_map/while/body/eval_jaxpr/ppermute | solution.py:11
  162.4 6.4 %collective-permute-start.1 = (f32[2,16,512]{2,1,0:T(8,128)}, f32[2,16,512]{2,1,0:T(8,128)S(1)}, u32[]{:S(2)}, u32[]{:S(2)}) collective-permute-start(f32[2,16,512]{2,1,0:T(8,128)} %get-tuple-element.103), channel_id=1, source_target_pairs={{4,0},{8,4},{12,8},{16,12},{20,16},{24,20},{28,24},{5,1},{9,5},{13... | collective-permute-start | bytes 196616 | tf_op jit(solution)/shard_map/while/body/eval_jaxpr/ppermute | solution.py:11
  170.3 5.5 %collective-permute-start = (f32[2,16,512]{2,1,0:T(8,128)}, f32[2,16,512]{2,1,0:T(8,128)S(1)}, u32[]{:S(2)}, u32[]{:S(2)}) collective-permute-start(f32[2,16,512]{2,1,0:T(8,128)} %get-tuple-element.102), channel_id=1, source_target_pairs={{0,4},{4,8},{8,12},{12,16},{16,20},{20,24},{24,28},{1,5},{5,9},{9,... | collective-permute-start | bytes 196616 | tf_op jit(solution)/shard_map/while/body/eval_jaxpr/ppermute | solution.py:11
  173.6 6.4 %collective-permute-start.1 = (f32[2,16,512]{2,1,0:T(8,128)}, f32[2,16,512]{2,1,0:T(8,128)S(1)}, u32[]{:S(2)}, u32[]{:S(2)}) collective-permute-start(f32[2,16,512]{2,1,0:T(8,128)} %get-tuple-element.103), channel_id=1, source_target_pairs={{4,0},{8,4},{12,8},{16,12},{20,16},{24,20},{28,24},{5,1},{9,5},{13... | collective-permute-start | bytes 196616 | tf_op jit(solution)/shard_map/while/body/eval_jaxpr/ppermute | solution.py:11
  180.0 2.7 copy-start.2
  182.7 5.4 %copy-start.4 = (f32[1024,512]{1,0:T(8,128)S(1)}, f32[1024,512]{1,0:T(8,128)}, u32[]{:S(2)}) copy-start(f32[1024,512]{1,0:T(8,128)} %reduce-scatter.3.cloned.1.call-done) | copy-start | bytes 6291460
  182.7 5.4 %copy-start.5 = (bf16[1024,512]{1,0:T(8,128)(2,1)S(1)}, bf16[1024,512]{1,0:T(8,128)(2,1)}, u32[]{:S(2)}) copy-start(bf16[1024,512]{1,0:T(8,128)(2,1)} %param.10) | copy-start | bytes 3145732
  190.1 324.8 %reduce-scatter.5.cloned.1.call-start = ((), (), s32[]{:S(2)}) async-start(), calls=%async_computation.4 | async-start | bytes 18874368 | tf_op jit(solution)/shard_map/reduce_scatter | solution.py:92
  232.0 0.7 copy-start.11
  232.0 2.5 copy-start.3
  234.5 3.7 copy-start.7
  234.6 3.7 copy-start.9
Sparse Core Ops, SparseCore 0:
  18.8 74.4 reduce-scatter.2
  190.2 31.3 all-gather.1
  232.1 282.7 reduce-scatter.4
where the time goes:
time: 522 us; the launch traced here: 521 us
  waiting for transfers between devices  404 us (77%)
  matrix products  42.5 us (8%)
  starting transfers between devices  35.8 us (7%)
  other arithmetic  19.5 us (4%)
  between operations  15.3 us (3%)
    reduce_scatter x1, waiting for transfers between devices, local(): lax.psum_scatter(jnp.dot(row_block, out_cotangent, preferred_element_type...  275 us
    reduce_scatter x1, waiting for transfers between devices, local(): lax.psum_scatter(lax.dot_general(row_block, out_cotangent, (((1,), (1,)),...  62.4 us
    ppermute x14, waiting for transfers between devices, passed_along(): return lax.ppermute(block, axis, route)  35.5 us
    ppermute x14, starting transfers between devices, passed_along(): return lax.ppermute(block, axis, route)  35.3 us
    all_gather x1, waiting for transfers between devices, local(): gathered = lax.all_gather(gated, 'ch', axis=0, tiled=True)  31.3 us
    add x7, other arithmetic, chain_turn(): transit[:, :, None] * behind + backward_part  11.1 us
  transfers between devices with their start and end apart: 17, of which 17 were waited for; matrix products, arithmetic and copies ran while one was open for 3% of the time, Pallas kernels for 0%

commit v1 on v0

--- a/solution.py
+++ b/solution.py
@@ -86,7 +86,9 @@
     query_grad = (output_grad * filtered).astype(jnp.bfloat16)
     key_grad = (spread * value_f).astype(jnp.bfloat16)
     value_grad = (spread * key_f).astype(jnp.bfloat16)
-    gathered = lax.all_gather(gated, "ch", axis=0, tiled=True)
+    gathered = jnp.concatenate(
+        lax.all_to_all(jnp.stack([gated] * lax.axis_size("ch")), "ch", 0, 0), axis=0
+    )
     norm_factor = 1.0 / math.sqrt(length * lax.axis_size("ctx"))
     row_block = gathered
     weight_grad = lax.psum_scatter(

time: 522 us -> 537 us (1.029)
  blocking collectives: 0 us -> 50.7 us
  waiting for transfers between devices: 404 us -> 370 us
    all_to_all x0 -> x1, blocking collectives: none -> 50.7 us  [local(): lax.all_to_all(jnp.stack([gated] * lax.axis_size('ch')), 'ch', 0, 0)]
    all_gather x1 -> x0, waiting for transfers between devices: 31.3 us -> none  [local(): gathered = lax.all_gather(gated, 'ch', axis=0, tiled=True)]
  transfers between devices with their start and end apart: 17 -> 16, of which waited for: 17 -> 16; matrix products, arithmetic and copies ran while one was open for 3% -> 3% of each run, Pallas kernels for 0% -> 0%
where the time goes in v1:
time: 537 us; the launch traced here: 536 us
  waiting for transfers between devices  370 us (69%)
  blocking collectives  50.7 us (9%)
  matrix products  40.3 us (8%)
  starting transfers between devices  35.6 us (7%)
  other arithmetic  19.3 us (4%)
  between operations  15.6 us (3%)
    reduce_scatter x1, waiting for transfers between devices, local(): lax.psum_scatter(jnp.dot(row_block, out_cotangent, preferred_element_type...  272 us
    reduce_scatter x1, waiting for transfers between devices, local(): lax.psum_scatter(lax.dot_general(row_block, out_cotangent, (((1,), (1,)),...  62.4 us
    all_to_all x1, blocking collectives, local(): lax.all_to_all(jnp.stack([gated] * lax.axis_size('ch')), 'ch', 0, 0)  50.7 us
    ppermute x14, waiting for transfers between devices, passed_along(): return lax.ppermute(block, axis, route)  35.5 us
    ppermute x14, starting transfers between devices, passed_along(): return lax.ppermute(block, axis, route)  35.3 us
    add x7, other arithmetic, chain_turn(): transit[:, :, None] * behind + backward_part  11.2 us
  transfers between devices with their start and end apart: 16, of which 16 were waited for; matrix products, arithmetic and copies ran while one was open for 3% of the time, Pallas kernels for 0%

profile of v1, /device:TPU:0, one launch (start us, length us, event | category | flops | bytes accessed | tf_op | source)
XLA Modules:
  0.0 535.8 jit_solution(3834917065892836863)
XLA Ops:
  7.2 1.2 copy-done
  8.4 10.2 %fusion.70 = f32[4096,512]{1,0:T(8,128)} fusion(bf16[4096,1024]{1,0:T(8,128)(2,1)} %param.16, bf16[512,1024]{1,0:T(8,128)(2,1)S(1)} %copy-done), kind=kOutput, calls=%fused_computation.83 | convolution fusion | flops 4294967296 | bytes 17825792 | tf_op jit(solution)/shard_map/dot_general | solution.py:28
  23.4 3.3 fusion.37
  27.1 1.3 copy-done.1
  28.4 2.5 fusion.33
  30.9 62.4 %reduce-scatter.3.cloned.1.call-done = f32[1024,512]{1,0:T(8,128)} async-done(((f32[4096,512]{1,0:T(8,128)}), f32[1024,512]{1,0:T(8,128)}) %reduce-scatter.3.cloned.1.call-update) | async-done | bytes 2097168 | tf_op jit(solution)/shard_map/reduce_scatter | solution.py:27
  93.3 2.2 convert_multiply_fusion.1
  95.4 2.5 fusion.29
  97.9 82.1 %while.12 = (s32[]{:T(128)}, f32[2,16,512]{2,1,0:T(8,128)S(1)}, f32[2,16,512]{2,1,0:T(8,128)S(1)}, f32[2,16]{1,0:T(2,128)S(1)}, f32[2,16,512]{2,1,0:T(8,128)}, /*index=5*/f32[2,16,512]{2,1,0:T(8,128)}, s32[]{:T(128)}) while((s32[]{:T(128)}, f32[2,16,512]{2,1,0:T(8,128)S(1)}, f32[2,16,512]{2,1,0:T(8,128)S(1)}, f32[2,16]{1,0:T(2,128)S(1)}, ...), condition=%wide.region_4.5_spmd, body=%wide.region_3.4_spmd.sunk | while | flops 65538 | bytes 917789 | solution.py:78
  97.9 1.6 multiply_add_fusion.3
  99.5 3.3 collective-permute-start
  102.9 1.3 collective-permute-start.1
  104.2 0.9 collective-permute-done
  105.1 4.2 collective-permute-done.1
  109.3 1.6 multiply_add_fusion.3
  110.9 4.3 collective-permute-start
  115.2 1.3 collective-permute-start.1
  117.4 4.2 collective-permute-done.1
  121.5 1.6 multiply_add_fusion.3
  123.1 3.4 collective-permute-start
  126.5 1.3 collective-permute-start.1
  127.8 1.5 collective-permute-done
  129.3 3.6 collective-permute-done.1
  132.9 1.6 multiply_add_fusion.3
  134.5 4.3 collective-permute-start
  138.7 1.3 collective-permute-start.1
  140.9 4.2 collective-permute-done.1
  145.1 1.6 multiply_add_fusion.3
  146.7 3.4 collective-permute-start
  150.1 1.3 collective-permute-start.1
  152.3 4.2 collective-permute-done.1
  156.4 1.6 multiply_add_fusion.3
  158.0 4.4 collective-permute-start
  162.4 1.3 collective-permute-start.1
  164.6 4.2 collective-permute-done.1
  168.8 1.6 multiply_add_fusion.3
  170.4 3.3 collective-permute-start
  173.6 1.3 collective-permute-start.1
  175.9 4.2 collective-permute-done.1
  180.0 2.7 fusion.24
  182.8 5.4 %fusion.8 = f32[2,512,512]{2,1,0:T(8,128)S(1)} fusion(f32[2,512,512]{2,1,0:T(8,128)S(1)} %fusion.24, f32[2,512,512]{2,1,0:T(8,128)S(1)} %bitcast.25, f32[2,512,512]{2,1,0:T(8,128)} %fusion.37, pred[512,512]{1,0:T(8,128)(4,1)S(1)} %fusion.16), kind=kOutput, calls=%fused_computation.17 | convolution fusion | flops 3222274048 | bytes 8650752 | tf_op jit(solution)/shard_map/gcs,gts->gct/dot_general | solution.py:79
  188.2 1.7 fusion.2
  190.3 50.7 %all_to_all.5 = bf16[4,1024,512]{2,1,0:T(8,128)(2,1)S(1)} all-to-all(bf16[4,1024,512]{2,1,0:T(8,128)(2,1)S(1)} %stack.2), channel_id=1, replica_groups=mesh['ctx'=8,'ch'=4] {'ch'}, dimensions={0} | all-to-all | bytes 8388608 | tf_op jit(solution)/shard_map/all_to_all | solution.py:90
  241.0 8.1 %broadcast_multiply_fusion = f32[4096,1024]{1,0:T(8,128)} fusion(bf16[4096,512]{1,0:T(8,128)(2,1)S(1)} %bitcast.26, bf16[512,1024]{1,0:T(8,128)(2,1)S(1)} %copy-done), kind=kOutput, calls=%fused_computation.2 | convolution fusion | flops 4299161600 | bytes 22020096 | tf_op jit(solution)/shard_map/dot_general | solution.py:95
  249.8 1.9 fusion.19
  251.7 3.7 fusion.11
  255.4 1.8 fusion
  257.2 271.7 %reduce-scatter.5.cloned.1.call-done = f32[512,1024]{1,0:T(8,128)} async-done(((f32[4096,1024]{1,0:T(8,128)}), f32[512,1024]{1,0:T(8,128)}) %reduce-scatter.5.cloned.1.call-update) | async-done | bytes 2097168 | tf_op jit(solution)/shard_map/reduce_scatter | solution.py:94
  (51 shorter events, 9.2 us)
Async XLA Ops:
  7.2 1.2 copy-start
  7.2 86.1 %reduce-scatter.3.cloned.1.call-start = ((), (), s32[]{:S(2)}) async-start(), calls=%async_computation.3 | async-start | bytes 10485760 | tf_op jit(solution)/shard_map/reduce_scatter | solution.py:27
  18.6 0.7 copy-start.13
  18.6 3.9 copy-start.12
  18.6 4.8 copy-start.10
  18.7 8.1 %copy-start.6 = (bf16[1024,512]{1,0:T(8,128)(2,1)S(1)}, bf16[1024,512]{1,0:T(8,128)(2,1)}, u32[]{:S(2)}) copy-start(bf16[1024,512]{1,0:T(8,128)(2,1)} %param.12) | copy-start | bytes 3145732
  18.7 8.1 %copy-start.8 = (bf16[1024,512]{1,0:T(8,128)(2,1)S(1)}, bf16[1024,512]{1,0:T(8,128)(2,1)}, u32[]{:S(2)}) copy-start(bf16[1024,512]{1,0:T(8,128)(2,1)} %param.11) | copy-start | bytes 3145732
  18.7 510.2 %reduce-scatter.5.cloned.1.call-start = ((), (), s32[]{:S(2)}) async-start(), calls=%async_computation.4 | async-start | bytes 18874368 | tf_op jit(solution)/shard_map/reduce_scatter | solution.py:94
  27.1 1.3 copy-start.1
  99.5 5.6 %collective-permute-start = (f32[2,16,512]{2,1,0:T(8,128)}, f32[2,16,512]{2,1,0:T(8,128)S(1)}, u32[]{:S(2)}, u32[]{:S(2)}) collective-permute-start(f32[2,16,512]{2,1,0:T(8,128)} %get-tuple-element.102), channel_id=1, source_target_pairs={{0,4},{4,8},{8,12},{12,16},{16,20},{20,24},{24,28},{1,5},{5,9},{9,... | collective-permute-start | bytes 196616 | tf_op jit(solution)/shard_map/while/body/eval_jaxpr/ppermute | solution.py:11
  102.9 6.4 %collective-permute-start.1 = (f32[2,16,512]{2,1,0:T(8,128)}, f32[2,16,512]{2,1,0:T(8,128)S(1)}, u32[]{:S(2)}, u32[]{:S(2)}) collective-permute-start(f32[2,16,512]{2,1,0:T(8,128)} %get-tuple-element.103), channel_id=1, source_target_pairs={{4,0},{8,4},{12,8},{16,12},{20,16},{24,20},{28,24},{5,1},{9,5},{13... | collective-permute-start | bytes 196616 | tf_op jit(solution)/shard_map/while/body/eval_jaxpr/ppermute | solution.py:11
  110.9 6.5 %collective-permute-start = (f32[2,16,512]{2,1,0:T(8,128)}, f32[2,16,512]{2,1,0:T(8,128)S(1)}, u32[]{:S(2)}, u32[]{:S(2)}) collective-permute-start(f32[2,16,512]{2,1,0:T(8,128)} %get-tuple-element.102), channel_id=1, source_target_pairs={{0,4},{4,8},{8,12},{12,16},{16,20},{20,24},{24,28},{1,5},{5,9},{9,... | collective-permute-start | bytes 196616 | tf_op jit(solution)/shard_map/while/body/eval_jaxpr/ppermute | solution.py:11
  115.2 6.4 %collective-permute-start.1 = (f32[2,16,512]{2,1,0:T(8,128)}, f32[2,16,512]{2,1,0:T(8,128)S(1)}, u32[]{:S(2)}, u32[]{:S(2)}) collective-permute-start(f32[2,16,512]{2,1,0:T(8,128)} %get-tuple-element.103), channel_id=1, source_target_pairs={{4,0},{8,4},{12,8},{16,12},{20,16},{24,20},{28,24},{5,1},{9,5},{13... | collective-permute-start | bytes 196616 | tf_op jit(solution)/shard_map/while/body/eval_jaxpr/ppermute | solution.py:11
  123.1 6.2 %collective-permute-start = (f32[2,16,512]{2,1,0:T(8,128)}, f32[2,16,512]{2,1,0:T(8,128)S(1)}, u32[]{:S(2)}, u32[]{:S(2)}) collective-permute-start(f32[2,16,512]{2,1,0:T(8,128)} %get-tuple-element.102), channel_id=1, source_target_pairs={{0,4},{4,8},{8,12},{12,16},{16,20},{20,24},{24,28},{1,5},{5,9},{9,... | collective-permute-start | bytes 196616 | tf_op jit(solution)/shard_map/while/body/eval_jaxpr/ppermute | solution.py:11
  126.5 6.4 %collective-permute-start.1 = (f32[2,16,512]{2,1,0:T(8,128)}, f32[2,16,512]{2,1,0:T(8,128)S(1)}, u32[]{:S(2)}, u32[]{:S(2)}) collective-permute-start(f32[2,16,512]{2,1,0:T(8,128)} %get-tuple-element.103), channel_id=1, source_target_pairs={{4,0},{8,4},{12,8},{16,12},{20,16},{24,20},{28,24},{5,1},{9,5},{13... | collective-permute-start | bytes 196616 | tf_op jit(solution)/shard_map/while/body/eval_jaxpr/ppermute | solution.py:11
  134.5 6.5 %collective-permute-start = (f32[2,16,512]{2,1,0:T(8,128)}, f32[2,16,512]{2,1,0:T(8,128)S(1)}, u32[]{:S(2)}, u32[]{:S(2)}) collective-permute-start(f32[2,16,512]{2,1,0:T(8,128)} %get-tuple-element.102), channel_id=1, source_target_pairs={{0,4},{4,8},{8,12},{12,16},{16,20},{20,24},{24,28},{1,5},{5,9},{9,... | collective-permute-start | bytes 196616 | tf_op jit(solution)/shard_map/while/body/eval_jaxpr/ppermute | solution.py:11
  138.7 6.4 %collective-permute-start.1 = (f32[2,16,512]{2,1,0:T(8,128)}, f32[2,16,512]{2,1,0:T(8,128)S(1)}, u32[]{:S(2)}, u32[]{:S(2)}) collective-permute-start(f32[2,16,512]{2,1,0:T(8,128)} %get-tuple-element.103), channel_id=1, source_target_pairs={{4,0},{8,4},{12,8},{16,12},{20,16},{24,20},{28,24},{5,1},{9,5},{13... | collective-permute-start | bytes 196616 | tf_op jit(solution)/shard_map/while/body/eval_jaxpr/ppermute | solution.py:11
  146.7 5.6 %collective-permute-start = (f32[2,16,512]{2,1,0:T(8,128)}, f32[2,16,512]{2,1,0:T(8,128)S(1)}, u32[]{:S(2)}, u32[]{:S(2)}) collective-permute-start(f32[2,16,512]{2,1,0:T(8,128)} %get-tuple-element.102), channel_id=1, source_target_pairs={{0,4},{4,8},{8,12},{12,16},{16,20},{20,24},{24,28},{1,5},{5,9},{9,... | collective-permute-start | bytes 196616 | tf_op jit(solution)/shard_map/while/body/eval_jaxpr/ppermute | solution.py:11
  150.1 6.4 %collective-permute-start.1 = (f32[2,16,512]{2,1,0:T(8,128)}, f32[2,16,512]{2,1,0:T(8,128)S(1)}, u32[]{:S(2)}, u32[]{:S(2)}) collective-permute-start(f32[2,16,512]{2,1,0:T(8,128)} %get-tuple-element.103), channel_id=1, source_target_pairs={{4,0},{8,4},{12,8},{16,12},{20,16},{24,20},{28,24},{5,1},{9,5},{13... | collective-permute-start | bytes 196616 | tf_op jit(solution)/shard_map/while/body/eval_jaxpr/ppermute | solution.py:11
  158.0 6.6 %collective-permute-start = (f32[2,16,512]{2,1,0:T(8,128)}, f32[2,16,512]{2,1,0:T(8,128)S(1)}, u32[]{:S(2)}, u32[]{:S(2)}) collective-permute-start(f32[2,16,512]{2,1,0:T(8,128)} %get-tuple-element.102), channel_id=1, source_target_pairs={{0,4},{4,8},{8,12},{12,16},{16,20},{20,24},{24,28},{1,5},{5,9},{9,... | collective-permute-start | bytes 196616 | tf_op jit(solution)/shard_map/while/body/eval_jaxpr/ppermute | solution.py:11
  162.4 6.4 %collective-permute-start.1 = (f32[2,16,512]{2,1,0:T(8,128)}, f32[2,16,512]{2,1,0:T(8,128)S(1)}, u32[]{:S(2)}, u32[]{:S(2)}) collective-permute-start(f32[2,16,512]{2,1,0:T(8,128)} %get-tuple-element.103), channel_id=1, source_target_pairs={{4,0},{8,4},{12,8},{16,12},{20,16},{24,20},{28,24},{5,1},{9,5},{13... | collective-permute-start | bytes 196616 | tf_op jit(solution)/shard_map/while/body/eval_jaxpr/ppermute | solution.py:11
  170.4 5.5 %collective-permute-start = (f32[2,16,512]{2,1,0:T(8,128)}, f32[2,16,512]{2,1,0:T(8,128)S(1)}, u32[]{:S(2)}, u32[]{:S(2)}) collective-permute-start(f32[2,16,512]{2,1,0:T(8,128)} %get-tuple-element.102), channel_id=1, source_target_pairs={{0,4},{4,8},{8,12},{12,16},{16,20},{20,24},{24,28},{1,5},{5,9},{9,... | collective-permute-start | bytes 196616 | tf_op jit(solution)/shard_map/while/body/eval_jaxpr/ppermute | solution.py:11
  173.6 6.4 %collective-permute-start.1 = (f32[2,16,512]{2,1,0:T(8,128)}, f32[2,16,512]{2,1,0:T(8,128)S(1)}, u32[]{:S(2)}, u32[]{:S(2)}) collective-permute-start(f32[2,16,512]{2,1,0:T(8,128)} %get-tuple-element.103), channel_id=1, source_target_pairs={{4,0},{8,4},{12,8},{16,12},{20,16},{24,20},{28,24},{5,1},{9,5},{13... | collective-permute-start | bytes 196616 | tf_op jit(solution)/shard_map/while/body/eval_jaxpr/ppermute | solution.py:11
  180.0 2.7 copy-start.2
  182.7 5.5 %copy-start.4 = (f32[1024,512]{1,0:T(8,128)S(1)}, f32[1024,512]{1,0:T(8,128)}, u32[]{:S(2)}) copy-start(f32[1024,512]{1,0:T(8,128)} %reduce-scatter.3.cloned.1.call-done) | copy-start | bytes 6291460
  182.7 5.5 %copy-start.5 = (bf16[1024,512]{1,0:T(8,128)(2,1)S(1)}, bf16[1024,512]{1,0:T(8,128)(2,1)}, u32[]{:S(2)}) copy-start(bf16[1024,512]{1,0:T(8,128)(2,1)} %param.10) | copy-start | bytes 3145732
  249.1 0.7 copy-start.11
  249.1 2.5 copy-start.3
  251.6 3.7 copy-start.7
  251.7 3.7 copy-start.9
Sparse Core Ops, SparseCore 0:
  18.8 74.4 reduce-scatter.2
  249.2 279.6 reduce-scatter.4
